TPU v7x, 32 devices: a whole 2x2x4 slice. The times are simulated.
32 devices in a mesh: dp: 4 (over y, x), mp: 8 (over z, core).
Axes of the slice: x: 2, y: 2, z: 4, core: 2. Of those that a mesh axis runs over, the one named last changes fastest.
Arguments:
- train_acts: bfloat16 [512, 4096], P('dp', 'mp'), may hold values from -6 to 6
- train_grads: bfloat16 [512, 7168], P('dp', 'mp'), may hold values from -0.75 to 0.75
- query_acts: bfloat16 [1024, 4096], P('dp', 'mp'), may hold values from -6 to 6
- query_grads: bfloat16 [1024, 7168], P('dp', 'mp'), may hold values from -0.75 to 0.75
- basis_in: bfloat16 [4096, 4096], P('mp'), may hold values from -0.125 to 0.125
- basis_out: bfloat16 [7168, 7168], P('mp'), may hold values from -0.09375 to 0.09375
- eigvals: bfloat16 [4096, 7168], P(None, 'mp'), may hold values from 0.25 to 4
Outputs:
- scores: float32 [16, 8], P(None, 'dp')
- energies: float32 [8], P('dp')
All inputs are finite; a program needn't handle non-finite values.
Results may differ from a plain program's by a relative error of at most 0.0048.
Values may be sent and summed in bfloat16 or wider, within the bound.
No kernel may reach another device: no remote copies, remote signals or barrier semaphores. Data moves between devices by JAX's collectives and lax.ppermute only.
A program may use at most 128 MiB of HBM per device.

v0:
```python
import math
import jax
import jax.numpy as jnp
from jax import lax
from jax.sharding import PartitionSpec as P

D = 4096
H = 7168
SEQ = 64
damping = 0.1


def pair_scores(query_a, query_g, scaled):
    applied = jnp.einsum("it,nij->ntj", query_a, scaled, preferred_element_type=jnp.float32)
    per_token = jnp.sum(applied * jnp.transpose(query_g).astype(jnp.float32)[None], axis=2)
    grouped = jnp.sum(per_token.reshape(per_token.shape[0], -1, SEQ), axis=2)
    return jnp.transpose(grouped)


def on_device(train_acts, train_grads, query_acts, query_grads, basis_in, basis_out, eigvals):
    train_rows = train_acts.shape[0]
    train_seqs = train_rows // SEQ
    acts = jnp.concatenate([train_acts, query_acts], axis=0)
    grads = jnp.concatenate([train_grads, query_grads], axis=0)
    columns = basis_in
    rot_acts = lax.psum(
        jnp.einsum("fc,rf->cr", columns, acts, preferred_element_type=jnp.float32), "mp"
    ).astype(jnp.bfloat16)
    columns = basis_out
    rot_grads = lax.psum_scatter(
        jnp.einsum("fc,rf->cr", columns, grads, preferred_element_type=jnp.float32),
        "mp",
        scatter_dimension=0,
        tiled=True,
    ).astype(jnp.bfloat16)
    train_a = rot_acts[:, :train_rows].reshape(rot_acts.shape[0], train_seqs, SEQ)
    train_g = rot_grads[:, :train_rows].reshape(rot_grads.shape[0], train_seqs, SEQ)
    query_a = rot_acts[:, train_rows:]
    query_g = rot_grads[:, train_rows:]
    train_outer = jnp.einsum("isk,jsk->sij", train_a, train_g, preferred_element_type=jnp.float32)
    shifted = eigvals.astype(jnp.float32) + damping
    scaled = (train_outer / shifted).astype(jnp.bfloat16)
    energy_part = jnp.sum(train_outer * train_outer, axis=(1, 2))
    all_query_a, all_query_g = (
        lax.all_gather(query_a, "dp", axis=1, tiled=True),
        lax.all_gather(query_g, "dp", axis=1, tiled=True),
    )
    partial_value = pair_scores(all_query_a, all_query_g, scaled)
    total_scores, total_energy = lax.psum((partial_value, energy_part), "mp")
    scores = total_scores * (1.0 / math.sqrt(D * H))
    energies = total_energy / (D * H)
    return (scores, energies)


def solution(mesh):
    return jax.shard_map(
        on_device,
        mesh=mesh,
        in_specs=(
            P("dp", "mp"),
            P("dp", "mp"),
            P("dp", "mp"),
            P("dp", "mp"),
            P("mp", None),
            P("mp", None),
            P(None, "mp"),
        ),
        out_specs=(P(None, "dp"), P("dp")),
        check_vma=False,
    )
```

profile of v0, /device:TPU:0, one launch (start us, length us, event | category | flops | bytes accessed | tf_op | source)
XLA Modules:
  0.0 401.3 jit_solution(1922817455804115351)
XLA Ops:
  7.2 0.0 reduce-scatter.2.cloned.1.call-start
  7.2 11.4 %convolution_bitcast_fusion = f32[7168,384]{0,1:T(8,128)} fusion(bf16[896,7168]{1,0:T(8,128)(2,1)} %param.12, bf16[256,896]{1,0:T(8,128)(2,1)} %param.10, bf16[128,896]{1,0:T(8,128)(2,1)} %param.8), kind=kOutput, calls=%fused_computation.4 | convolution fusion | flops 4933877760 | bytes 24543232 | tf_op jit(solution)/shard_map/fc,rf->cr/dot_general | solution.py:31
  18.7 0.0 copy-start.1
  18.7 0.0 copy-start.2
  18.7 0.0 reduce-scatter.2.cloned.1.call-update
  18.7 0.0 all-gather.5.cloned.1.call-start
  18.7 0.9 copy-done.1
  19.6 0.0 copy-done.2
  19.6 6.6 %convolution_bitcast_fusion.1 = f32[4096,384]{0,1:T(8,128)} fusion(bf16[512,4096]{1,0:T(8,128)(2,1)} %param.11, bf16[256,512]{1,0:T(8,128)(2,1)S(1)} %copy-done.1, bf16[128,512]{1,0:T(8,128)(2,1)S(1)} %copy-done.2), kind=kOutput, calls=%fused_computation.8 | convolution fusion | flops 1611399168 | bytes 10878976 | tf_op jit(solution)/shard_map/fc,rf->cr/dot_general | solution.py:27
  26.2 109.6 %reduce-scatter.2.cloned.1.call-done = f32[896,384]{0,1:T(8,128)} async-done(((f32[7168,384]{0,1:T(8,128)}), f32[896,384]{0,1:T(8,128)}) %reduce-scatter.2.cloned.1.call-update) | async-done | bytes 1376272 | tf_op jit(solution)/shard_map/reduce_scatter | solution.py:30
  135.8 1.4 convert_element_type.19
  137.3 0.0 copy-start
  137.3 0.8 copy-done
  138.1 0.8 slice.19
  138.9 0.0 all-gather.5.cloned.1.call-update
  138.9 0.0 all-gather.3.cloned.1.call-start
  139.0 127.1 %all-reduce.2 = bf16[4096,384]{0,1:T(8,128)(2,1)S(1)} all-reduce(f32[4096,384]{0,1:T(8,128)} %convolution_bitcast_fusion.1), channel_id=1, replica_groups=mesh['dp'=4,'mp'=8] {'mp'}, use_global_device_ids=true, to_apply=%region_0.0 | all-reduce | flops 1572864 | bytes 9437184 | tf_op jit(solution)/shard_map/psum | solution.py:26
  266.1 1.5 slice.18
  267.5 0.0 all-gather.3.cloned.1.call-update
  267.6 0.1 slice.16
  267.6 0.0 slice-start
  267.7 11.2 %convert_add_fusion = f32[4096,896]{1,0:T(8,128)} fusion(bf16[4096,896]{1,0:T(8,128)(2,1)} %param.13), kind=kLoop, calls=%fused_computation.2 | loop fusion | flops 7340032 | bytes 22020096 | tf_op jit(solution)/shard_map/add | solution.py:41
  278.8 0.0 slice-done
  278.8 12.1 %multiply_reduce_fusion = (f32[2]{0:T(128)S(1)}, f32[2,4096,896]{2,1,0:T(8,128)}) fusion(bf16[4096,2,64]{0,2,1:T(8,128)(2,1)S(1)} %bitcast.22, bf16[896,2,64]{0,2,1:T(8,128)(2,1)S(1)} %bitcast.23), kind=kOutput, calls=%fused_computation | convolution fusion | flops 954204160 | bytes 30638088 | tf_op jit(solution)/shard_map/isk,jsk->sij/dot_general | solution.py:40
  290.9 0.0 all-gather.5.cloned.1.call-done
  290.9 3.6 convert_bitcast_fusion
  294.5 5.0 %copy.14 = f32[1024,896]{0,1:T(8,128)} copy(f32[1024,896]{1,0:T(8,128)} %convert_bitcast_fusion) | data formatting | bytes 7340032 | tf_op jit(solution)/shard_map/convert_element_type | solution.py:15
  299.5 54.0 %all-gather.3.cloned.1.call-done = bf16[4096,1024]{0,1:T(8,128)(2,1)} async-done(((bf16[4096,256]{0,1:T(8,128)(2,1)}), bf16[4096,1024]{0,1:T(8,128)(2,1)}) %all-gather.3.cloned.1.call-update) | async-done | bytes 8388624 | tf_op jit(solution)/shard_map/all_gather | solution.py:45
  353.5 23.9 %fusion.2 = f32[2,1024]{1,0:T(2,128)S(1)} fusion(f32[1024,896]{0,1:T(8,128)} %copy.14, bf16[4096,1024]{0,1:T(8,128)(2,1)} %all-gather.3.cloned.1.call-done, f32[2,4096,896]{2,1,0:T(8,128)} %get-tuple-element.5, f32[4096,896]{1,0:T(8,128)} %convert_add_fusion), kind=kOutput, calls=%fused_computation.7 | convolution fusion | flops 15050733568 | bytes 56107008 | tf_op jit(solution)/shard_map/it,nij->ntj/dot_general | solution.py:14
  377.4 0.1 reshape.17
  377.5 0.1 reduce_sum.28
  377.6 16.2 %all-reduce = (f32[16,2]{0,1:T(2,128)S(1)}, f32[2]{0:T(128)S(1)}) all-reduce(f32[16,2]{0,1:T(2,128)S(1)} %bitcast.24, f32[2]{0:T(128)S(1)} %get-tuple-element.4), channel_id=1, replica_groups=mesh['dp'=4,'mp'=8] {'mp'}, use_global_device_ids=true, to_apply=%region_4.0 | all-reduce | flops 34 | bytes 272 | tf_op jit(solution)/shard_map/psum | solution.py:49
  393.7 0.6 broadcast_multiply_fusion
  394.3 0.5 broadcast_multiply_fusion.1
Async XLA Ops:
  7.2 128.7 %reduce-scatter.2.cloned.1.call-start = ((), (), s32[]{:S(2)}) async-start(), calls=%async_computation.1 | async-start | bytes 12386304 | tf_op jit(solution)/shard_map/reduce_scatter | solution.py:30
  18.7 0.9 copy-start.1
  18.7 1.0 copy-start.2
  18.7 272.2 %all-gather.5.cloned.1.call-start = ((), (), s32[]{:S(2)}) async-start(), calls=%async_computation.3 | async-start | bytes 2293760 | tf_op jit(solution)/shard_map/all_gather | solution.py:46
  137.3 0.9 copy-start
  138.9 214.6 %all-gather.3.cloned.1.call-start = ((), (), s32[]{:S(2)}) async-start(), calls=%async_computation.2 | async-start | bytes 10485760 | tf_op jit(solution)/shard_map/all_gather | solution.py:45
  267.6 11.2 %slice-start = ((bf16[896,384]{0,1:T(8,128)(2,1)}), bf16[896,128]{0,1:T(8,128)(2,1)S(1)}, s32[]{:S(2)}) async-start(bf16[896,384]{0,1:T(8,128)(2,1)} %copy-done), calls=%async_computation.4 | async-start | bytes 458752 | tf_op jit(solution)/shard_map/slice | solution.py:37
Sparse Core Ops, SparseCore 0:
  18.8 117.0 reduce-scatter.1
  139.1 31.4 all-gather.4
  267.7 85.7 all-gather.2
where the time goes:
time: 402 us; the launch traced here: 401 us
  waiting for transfers between devices  164 us (41%)
  blocking collectives  143 us (36%)
  matrix products  53.9 us (13%)
  other arithmetic  17.3 us (4%)
  between operations  13.8 us (3%)
  local copies, waits for them, and re-layouts  9.22 us (2%)
    psum x1, blocking collectives, on_device(): lax.psum(jnp.einsum('fc,rf->cr', columns, acts, preferred_element_type=jn...  127 us
    reduce_scatter x1, waiting for transfers between devices, on_device(): lax.psum_scatter(jnp.einsum('fc,rf->cr', columns, grads, preferred_elemen...  110 us
    all_gather x1, waiting for transfers between devices, on_device(): lax.all_gather(query_a, 'dp', axis=1, tiled=True)  54 us
    dot_general x1, matrix products, pair_scores(): jnp.einsum('it,nij->ntj', query_a, scaled, preferred_element_type=jnp.flo...  23.9 us
    psum x1, blocking collectives, on_device(): total_scores, total_energy = lax.psum((partial_value, energy_part), 'mp')  16.2 us
    dot_general x1, matrix products, on_device(): jnp.einsum('isk,jsk->sij', train_a, train_g, preferred_element_type=jnp.f...  12.1 us
    dot_general x1, matrix products, on_device(): jnp.einsum('fc,rf->cr', columns, grads, preferred_element_type=jnp.float32)  11.4 us
    add x1, other arithmetic, on_device(): shifted = eigvals.astype(jnp.float32) + damping  11.2 us
  transfers between devices with their start and end apart: 3, of which 2 were waited for; matrix products, arithmetic and copies ran while one was open for 10% of the time, Pallas kernels for 0%

commit v1 on v0

--- a/solution.py
+++ b/solution.py
@@ -8,6 +8,19 @@
 H = 7168
 SEQ = 64
 damping = 0.1
+
+
+def gather_around(x, axis, dim):
+    ways = lax.axis_size(axis)
+    up = [(d, (d + 1) % ways) for d in range(ways)]
+    down = [(d, (d - 1) % ways) for d in range(ways)]
+    earlier, later = ([x], [x])
+    for _ in range(ways // 2):
+        earlier.append(lax.ppermute(earlier[-1], axis, up))
+    for _ in range((ways - 1) // 2):
+        later.append(lax.ppermute(later[-1], axis, down))
+    line = jnp.concatenate([*earlier[::-1], *later[1:]], axis=dim)
+    return jnp.roll(line, (lax.axis_index(axis) - ways // 2) * x.shape[dim], axis=dim)
 
 
 def pair_scores(query_a, query_g, scaled):
@@ -42,7 +55,7 @@
     scaled = (train_outer / shifted).astype(jnp.bfloat16)
     energy_part = jnp.sum(train_outer * train_outer, axis=(1, 2))
     all_query_a, all_query_g = (
-        lax.all_gather(query_a, "dp", axis=1, tiled=True),
+        gather_around(query_a, "dp", 1),
         lax.all_gather(query_g, "dp", axis=1, tiled=True),
     )
     partial_value = pair_scores(all_query_a, all_query_g, scaled)

time: 402 us -> 494 us (1.23)
  blocking collectives: 143 us -> 245 us
  waiting for transfers between devices: 164 us -> 128 us
  local copies, waits for them, and re-layouts: 9.22 us -> 31.4 us
    ppermute x0 -> x3, waiting for transfers between devices: none -> 113 us  [the longest x2 80.5 us: gather_around(): earlier.append(lax.ppermute(earlier[-1], axis, up))]
    reduce_scatter x1, waiting for transfers between devices: 110 us -> 0.01 us  [on_device(): lax.psum_scatter(jnp.einsum('fc,rf->cr', columns, grads, preferred_elemen...]
    psum x1, blocking collectives: 127 us -> 229 us  [on_device(): lax.psum(jnp.einsum('fc,rf->cr', columns, acts, preferred_element_type=jn...]
    all_gather x1 -> x0, waiting for transfers between devices: 54 us -> none  [on_device(): lax.all_gather(query_a, 'dp', axis=1, tiled=True)]
    unnamed x6 -> x15, local copies, waits for them, and re-layouts: 1.76 us -> 19.8 us
    all_gather x1, waiting for transfers between devices: 0.01 us -> 15.4 us  [on_device(): lax.all_gather(query_g, 'dp', axis=1, tiled=True)]
  transfers between devices with their start and end apart: 3 -> 5, of which waited for: 2 -> 4; matrix products, arithmetic and copies ran while one was open for 10% -> 11% of each run, Pallas kernels for 0% -> 0%
where the time goes in v1:
time: 494 us; the launch traced here: 493 us
  blocking collectives  245 us (50%)
  waiting for transfers between devices  128 us (26%)
  matrix products  54.3 us (11%)
  local copies, waits for them, and re-layouts  31.4 us (6%)
  other arithmetic  15.7 us (3%)
  between operations  14.1 us (3%)
    psum x1, blocking collectives, on_device(): lax.psum(jnp.einsum('fc,rf->cr', columns, acts, preferred_element_type=jn...  229 us
    ppermute x2, waiting for transfers between devices, gather_around(): earlier.append(lax.ppermute(earlier[-1], axis, up))  80.5 us
    ppermute x1, waiting for transfers between devices, gather_around(): later.append(lax.ppermute(later[-1], axis, down))  32.4 us
    dot_general x1, matrix products, pair_scores(): jnp.einsum('it,nij->ntj', query_a, scaled, preferred_element_type=jnp.flo...  24 us
    unnamed x15, local copies, waits for them, and re-layouts  19.8 us
    psum x1, blocking collectives, on_device(): total_scores, total_energy = lax.psum((partial_value, energy_part), 'mp')  16.2 us
    all_gather x1, waiting for transfers between devices, on_device(): lax.all_gather(query_g, 'dp', axis=1, tiled=True)  15.4 us
    dot_general x1, matrix products, on_device(): jnp.einsum('isk,jsk->sij', train_a, train_g, preferred_element_type=jnp.f...  12.3 us
  transfers between devices with their start and end apart: 5, of which 4 were waited for; matrix products, arithmetic and copies ran while one was open for 11% of the time, Pallas kernels for 0%

profile of v1, /device:TPU:0, one launch (start us, length us, event | category | flops | bytes accessed | tf_op | source)
XLA Modules:
  0.0 493.1 jit_solution(12869374078021769901)
XLA Ops:
  7.2 0.0 copy-start.3
  7.2 0.0 copy-start.2
  7.2 0.0 reduce-scatter.2.cloned.1.call-start
  7.2 11.5 %convolution_bitcast_fusion = f32[7168,384]{0,1:T(8,128)} fusion(bf16[896,7168]{1,0:T(8,128)(2,1)} %param.12, bf16[256,896]{1,0:T(8,128)(2,1)} %param.10, bf16[128,896]{1,0:T(8,128)(2,1)} %param.8), kind=kOutput, calls=%fused_computation.4 | convolution fusion | flops 4933877760 | bytes 24543232 | tf_op jit(solution)/shard_map/fc,rf->cr/dot_general | solution.py:44
  18.7 0.0 reduce-scatter.2.cloned.1.call-update
  18.8 0.0 all-gather.2.cloned.1.call-start
  18.8 0.0 copy-done.3
  18.8 0.0 copy-done.2
  18.8 6.6 %convolution_bitcast_fusion.1 = f32[4096,384]{0,1:T(8,128)} fusion(bf16[512,4096]{1,0:T(8,128)(2,1)} %param.11, bf16[256,512]{1,0:T(8,128)(2,1)S(1)} %copy-done.2, bf16[128,512]{1,0:T(8,128)(2,1)S(1)} %copy-done.3), kind=kOutput, calls=%fused_computation.9 | convolution fusion | flops 1611399168 | bytes 10878976 | tf_op jit(solution)/shard_map/fc,rf->cr/dot_general | solution.py:40
  25.4 228.6 %all-reduce.2 = bf16[4096,384]{0,1:T(8,128)(2,1)S(1)} all-reduce(f32[4096,384]{0,1:T(8,128)} %convolution_bitcast_fusion.1), channel_id=1, replica_groups=mesh['dp'=4,'mp'=8] {'mp'}, use_global_device_ids=true, to_apply=%region_0.0 | all-reduce | flops 1572864 | bytes 9437184 | tf_op jit(solution)/shard_map/psum | solution.py:39
  254.0 1.6 slice.18
  255.6 1.5 collective-permute-start
  257.0 44.4 %collective-permute-done = bf16[4096,256]{0,1:T(8,128)(2,1)} collective-permute-done((bf16[4096,256]{0,1:T(8,128)(2,1)}, bf16[4096,256]{0,1:T(8,128)(2,1)}, u32[]{:S(2)}, u32[]{:S(2)}) %collective-permute-start) | collective-permute-done | bytes 2097184 | tf_op jit(solution)/shard_map/ppermute | solution.py:19
  301.4 1.4 collective-permute-start.1
  302.8 1.5 collective-permute-start.2
  304.3 9.6 %convert_add_fusion = f32[4096,896]{1,0:T(8,128)} fusion(bf16[4096,896]{1,0:T(8,128)(2,1)} %param.13), kind=kLoop, calls=%fused_computation.2 | loop fusion | flops 7340032 | bytes 22020096 | tf_op jit(solution)/shard_map/add | solution.py:54
  313.9 1.1 slice.16
  315.0 36.1 %collective-permute-done.1 = bf16[4096,256]{0,1:T(8,128)(2,1)} collective-permute-done((bf16[4096,256]{0,1:T(8,128)(2,1)}, bf16[4096,256]{0,1:T(8,128)(2,1)}, u32[]{:S(2)}, u32[]{:S(2)}) %collective-permute-start.1) | collective-permute-done | bytes 2097184 | tf_op jit(solution)/shard_map/ppermute | solution.py:19
  351.1 3.2 constant_dynamic-update-slice_fusion.7
  354.3 3.1 constant_dynamic-update-slice_fusion.6
  357.4 1.5 constant_dynamic-update-slice_fusion.5
  359.0 32.4 %collective-permute-done.2 = bf16[4096,256]{0,1:T(8,128)(2,1)} collective-permute-done((bf16[4096,256]{0,1:T(8,128)(2,1)}, bf16[4096,256]{0,1:T(8,128)(2,1)}, u32[]{:S(2)}, u32[]{:S(2)}) %collective-permute-start.2) | collective-permute-done | bytes 2097184 | tf_op jit(solution)/shard_map/ppermute | solution.py:21
  391.4 3.2 constant_dynamic-update-slice_fusion.4
  394.5 3.1 constant_dynamic-update-slice_fusion.3
  397.7 0.0 reduce-scatter.2.cloned.1.call-done
  397.7 1.4 convert_element_type.19
  399.1 0.0 copy-start.1
  399.1 0.9 copy-done.1
  399.9 0.8 slice.19
  400.7 0.0 slice-start
  400.7 0.0 all-gather.2.cloned.1.call-update
  400.8 0.0 copy-start
  400.8 3.2 constant_dynamic-update-slice_fusion.2
  404.0 1.6 constant_dynamic-update-slice_fusion.1
  405.6 3.1 constant_dynamic-update-slice_fusion
  408.7 0.0 slice-done
  408.7 0.0 copy-done
  408.7 12.3 %multiply_reduce_fusion = (f32[2]{0:T(128)S(1)}, f32[2,4096,896]{2,1,0:T(8,128)}) fusion(bf16[4096,2,64]{0,2,1:T(8,128)(2,1)S(1)} %bitcast.22, bf16[896,2,64]{0,2,1:T(8,128)(2,1)S(1)} %bitcast.23), kind=kOutput, calls=%fused_computation | convolution fusion | flops 954204160 | bytes 30638088 | tf_op jit(solution)/shard_map/isk,jsk->sij/dot_general | solution.py:53
  420.9 15.4 %all-gather.2.cloned.1.call-done = bf16[896,1024]{0,1:T(8,128)(2,1)} async-done(((bf16[896,256]{0,1:T(8,128)(2,1)}), bf16[896,1024]{0,1:T(8,128)(2,1)}) %all-gather.2.cloned.1.call-update) | async-done | bytes 1835024 | tf_op jit(solution)/shard_map/all_gather | solution.py:59
  436.3 3.5 convert_bitcast_fusion
  439.8 5.0 %copy.14 = f32[1024,896]{0,1:T(8,128)} copy(f32[1024,896]{1,0:T(8,128)} %convert_bitcast_fusion) | data formatting | bytes 7340032 | tf_op jit(solution)/shard_map/convert_element_type | solution.py:28
  444.8 24.0 %fusion.3 = f32[2,1024]{1,0:T(2,128)S(1)} fusion(f32[1024,896]{0,1:T(8,128)} %copy.14, bf16[4096,2048]{0,1:T(8,128)(2,1)} %constant_dynamic-update-slice_fusion, s32[]{:T(128)S(6)} %select_n.14, f32[2,4096,896]{2,1,0:T(8,128)} %get-tuple-element.5, f32[4096,896]{1,0:T(8,128)} %convert_add_fusion), kind=kOutput, calls=%fused_computation.8 | convolution fusion | flops 15050733568 | bytes 56107012 | tf_op jit(solution)/shard_map/it,nij->ntj/dot_general | solution.py:27
  468.8 0.1 reshape.17
  468.9 0.1 reduce_sum.28
  469.0 16.2 %all-reduce = (f32[16,2]{0,1:T(2,128)S(1)}, f32[2]{0:T(128)S(1)}) all-reduce(f32[16,2]{0,1:T(2,128)S(1)} %bitcast.24, f32[2]{0:T(128)S(1)} %get-tuple-element.4), channel_id=1, replica_groups=mesh['dp'=4,'mp'=8] {'mp'}, use_global_device_ids=true, to_apply=%region_4.5 | all-reduce | flops 34 | bytes 272 | tf_op jit(solution)/shard_map/psum | solution.py:62
  485.2 0.6 broadcast_multiply_fusion
  485.8 0.5 broadcast_multiply_fusion.1
Async XLA Ops:
  7.2 11.6 %copy-start.3 = (bf16[128,512]{1,0:T(8,128)(2,1)S(1)}, bf16[128,512]{1,0:T(8,128)(2,1)}, u32[]{:S(2)}) copy-start(bf16[128,512]{1,0:T(8,128)(2,1)} %param.7) | copy-start | bytes 393220
  7.2 11.6 %copy-start.2 = (bf16[256,512]{1,0:T(8,128)(2,1)S(1)}, bf16[256,512]{1,0:T(8,128)(2,1)}, u32[]{:S(2)}) copy-start(bf16[256,512]{1,0:T(8,128)(2,1)} %param.9) | copy-start | bytes 786436
  7.2 390.5 %reduce-scatter.2.cloned.1.call-start = ((), (), s32[]{:S(2)}) async-start(), calls=%async_computation.1 | async-start | bytes 12386304 | tf_op jit(solution)/shard_map/reduce_scatter | solution.py:43
  18.8 417.5 %all-gather.2.cloned.1.call-start = ((), (), s32[]{:S(2)}) async-start(), calls=%async_computation.2 | async-start | bytes 2293760 | tf_op jit(solution)/shard_map/all_gather | solution.py:59
  255.6 45.9 %collective-permute-start = (bf16[4096,256]{0,1:T(8,128)(2,1)}, bf16[4096,256]{0,1:T(8,128)(2,1)}, u32[]{:S(2)}, u32[]{:S(2)}) collective-permute-start(bf16[4096,256]{0,1:T(8,128)(2,1)} %slice.18), channel_id=1, source_target_pairs={{0,8},{8,16},{16,24},{24,0},{1,9},{9,17},{17,25},{25,1},{2,10},{10... | collective-permute-start | bytes 6291464 | tf_op jit(solution)/shard_map/ppermute | solution.py:19
  301.4 49.7 %collective-permute-start.1 = (bf16[4096,256]{0,1:T(8,128)(2,1)}, bf16[4096,256]{0,1:T(8,128)(2,1)}, u32[]{:S(2)}, u32[]{:S(2)}) collective-permute-start(bf16[4096,256]{0,1:T(8,128)(2,1)} %collective-permute-done), channel_id=1, source_target_pairs={{0,8},{8,16},{16,24},{24,0},{1,9},{9,17},{17,25},{25,1},{2,10},{10... | collective-permute-start | bytes 6291464 | tf_op jit(solution)/shard_map/ppermute | solution.py:19
  302.8 88.5 %collective-permute-start.2 = (bf16[4096,256]{0,1:T(8,128)(2,1)}, bf16[4096,256]{0,1:T(8,128)(2,1)}, u32[]{:S(2)}, u32[]{:S(2)}) collective-permute-start(bf16[4096,256]{0,1:T(8,128)(2,1)} %slice.18), channel_id=1, source_target_pairs={{0,24},{8,0},{16,8},{24,16},{1,25},{9,1},{17,9},{25,17},{2,26},{10... | collective-permute-start | bytes 6291464 | tf_op jit(solution)/shard_map/ppermute | solution.py:21
  399.1 0.9 copy-start.1
  400.7 7.9 %slice-start = ((bf16[896,384]{0,1:T(8,128)(2,1)}), bf16[896,128]{0,1:T(8,128)(2,1)S(1)}, s32[]{:S(2)}) async-start(bf16[896,384]{0,1:T(8,128)(2,1)} %copy-done.1), calls=%async_computation.3 | async-start | bytes 458752 | tf_op jit(solution)/shard_map/slice | solution.py:50
  400.8 7.9 %copy-start = (bf16[4096,128]{0,1:T(8,128)(2,1)S(1)}, bf16[4096,128]{0,1:T(8,128)(2,1)}, u32[]{:S(2)}) copy-start(bf16[4096,128]{0,1:T(8,128)(2,1)} %slice.16) | copy-start | bytes 3145732
Sparse Core Ops, SparseCore 0:
  18.9 212.7 reduce-scatter.1
  400.9 35.3 all-gather.1
